TPU v7x, 32 devices: a whole 2x2x4 slice. The times are simulated.
32 devices in a mesh: mesh: 32 (over z, y, x, core).
Axes of the slice: x: 2, y: 2, z: 4, core: 2. Of those that a mesh axis runs over, the one named last changes fastest.
Arguments:
- states: float32 [196608, 256], P('mesh'), may hold values from -30 to 30
- inv_sqrt_mass: float32 [196608], P('mesh'), may hold values from 0.25 to 1.75
- element_blocks: bfloat16 [512, 512, 512], P('mesh'), may hold values from -0.25 to 0.25
- element_nodes: int32 [512, 512], P('mesh'), may hold values from 0 to 6143, as said below
- element_counts: int32 [32], P('mesh'), may hold values from 1 to 16, as said below
- node_counts: int32 [32], replicated, may hold values from 4608 to 6144, as said below
- boundary_rows: int32 [32, 2, 384], P('mesh'), may hold values from 0 to 4607, as said below
Outputs:
- rotated: float32 [196608, 256], P('mesh')
Inputs may be any that keep to these rules, and one draw needn't show every extreme that they name: `node_counts`: live node rows of each device; some device has 6144. `element_counts`: live element slots of each device (the first slots are live); some device has 16. `element_nodes`: every entry is below its device's node count. `boundary_rows`: for each device the 768 entries are distinct rows below 4608.
All inputs are finite; a program needn't handle non-finite values.
Results may differ from a plain program's by a relative error of at most 0.0077.
Values sent between devices are 32-bit elements; how exact they have to be, the bound alone decides.
A program may use at most 128 MiB of HBM per device.

v0:
```python
import jax
import jax.numpy as jnp
from jax import lax
from jax.sharding import PartitionSpec as P


def passed_along(block, axis, distance):
    devices = range(lax.axis_size(axis))
    route = [(i - distance, i) for i in devices if i - distance in devices]
    return lax.ppermute(block, axis, route)


def body(
    states, inv_sqrt_mass, element_blocks, element_nodes, element_counts, node_counts, boundary_rows
):
    position = lax.axis_index("mesh")
    devices = lax.axis_size("mesh")
    row_total = states.shape[0]
    width = states.shape[1]
    slots = element_blocks.shape[0]
    lower_rows = boundary_rows[0, 0]
    upper_rows = boundary_rows[0, 1]
    shared = lower_rows.shape[0]
    has_below = position >= 1
    owner_vals, owner_mass = passed_along(
        (states[upper_rows], inv_sqrt_mass[upper_rows]), "mesh", 1
    )
    field = states.at[lower_rows].set(jnp.where(has_below, owner_vals, states[lower_rows]))
    mass = inv_sqrt_mass.at[lower_rows].set(
        jnp.where(has_below, owner_mass, inv_sqrt_mass[lower_rows])
    )
    live_slots = element_counts[0]
    row_index = jnp.arange(row_total)
    slot_index = jnp.arange(slots)
    slot_live = slot_index < live_slots

    def ham(values):
        scaled = (mass[:, None] * values).astype(jnp.bfloat16)
        empty = jnp.zeros((row_total, width), jnp.float32)

        def add_element(slot, total):
            rows = element_nodes[slot]

            def compute(acc):
                part = jnp.dot(
                    element_blocks[slot], scaled[rows], preferred_element_type=jnp.float32
                )
                return acc.at[rows].add(part)

            return lax.cond(slot_live[slot], compute, lambda acc: acc, total)

        local = lax.fori_loop(0, slots, add_element, empty)
        coming_up = passed_along(local[upper_rows], "mesh", 1)
        coming_down = passed_along(local[lower_rows], "mesh", -1)
        assembled = local.at[lower_rows].add(coming_up).at[upper_rows].add(coming_down)
        return mass[:, None] * assembled

    center = 0.5
    half_width = 1.5
    first = (ham(field) - center * field) / half_width
    second = 2.0 * (ham(first) - center * first) / half_width - field
    filtered = 2.0 * (ham(second) - center * second) / half_width - first
    live = row_index < node_counts[position]
    in_lower = jnp.any(row_index[:, None] == lower_rows[None, :], axis=1)
    owned = live & jnp.logical_not(in_lower & has_below)
    weighted = jnp.where(owned[:, None], filtered, 0.0)
    partial_value = lax.dot_general(
        weighted,
        weighted,
        (((0,), (0,)), ((), ())),
        precision=lax.Precision.HIGHEST,
        preferred_element_type=jnp.float32,
    )
    gram = lax.psum(partial_value, "mesh")
    total = (jnp.sum(node_counts) - shared * (devices - 1)).astype(jnp.float32)
    gram = gram / total
    factor = jnp.linalg.cholesky(gram)
    inverse = jax.scipy.linalg.solve_triangular(
        factor, jnp.eye(width, dtype=jnp.float32), lower=True
    )
    rotated = jnp.dot(
        filtered, inverse.T, precision=lax.Precision.HIGHEST, preferred_element_type=jnp.float32
    )
    return jnp.where(live[:, None], rotated, 0.0)


def solution(mesh):
    in_specs = (
        P("mesh", None),
        P("mesh"),
        P("mesh", None, None),
        P("mesh", None),
        P("mesh"),
        P(),
        P("mesh", None, None),
    )
    out_specs = P("mesh", None)
    return jax.shard_map(body, mesh=mesh, in_specs=in_specs, out_specs=out_specs, check_vma=False)
```

profile of v0, /device:TPU:0, one launch (start us, length us, event | category | flops | bytes accessed | tf_op | source)
XLA Modules:
  0.0 1117.1 jit_solution(17529059180484307456)
XLA Ops:
  7.3 5.8 copy.66
  13.1 2.5 gather_fusion.3
  18.1 4.4 gather_fusion.5
  22.5 4.5 collective-permute-start.1
  30.3 3.0 scatter_fusion.3
  33.3 9.7 scatter_custom_fusion.4
  43.0 3.3 multiply_convert_fusion.2
  46.4 3.1 broadcast.221.clone.1
  49.4 75.4 %while.49 = (s32[]{:T(128)}, f32[6144,256]{1,0:T(8,128)}, pred[16]{0:T(512)(128)(4,1)S(1)}, s32[16,512]{1,0:T(8,128)}, bf16[16,512,512]{2,1,0:T(8,128)(2,1)}, /*index=5*/bf16[6144,256]{1,0:T(8,128)(2,1)S(1)}, s32[]{:T(128)}) while((s32[]{:T(128)}, f32[6144,256]{1,0:T(8,128)}, pred[16]{0:T(512)(128)(4,1)S(1)}, s32[16,512]{1,0:T(8,128)}, ...), condition=%wide.region_6.7_spmd, body=%wide.region_2.6_spmd.sunk | while | flops 134351360 | bytes 3422386 | solution.py:52
  50.7 13.8 %conditional.6 = (f32[6144,256]{1,0:T(8,128)}) conditional(s32[]{:T(128)} %bitcast.62, f32[6144,256]{1,0:T(8,128)} %get-tuple-element.664, (s32[16,512]{1,0:T(8,128)}, s32[]{:T(128)}, bf16[16,512,512]{2,1,0:T(8,128)(2,1)}, bf16[6144,256]{1,0:T(8,128)(2,1)S(1)}, f32[6144,256]{1,0:T(8,128)}) %tuple.128), branch_computations={%region_3.3_spmd, %region_4.5_spmd} | conditional | flops 134351360 | bytes 3422258 | solution.py:50
  55.5 8.9 scatter_fusion
  65.7 13.8 %conditional.6 = (f32[6144,256]{1,0:T(8,128)}) conditional(s32[]{:T(128)} %bitcast.62, f32[6144,256]{1,0:T(8,128)} %get-tuple-element.664, (s32[16,512]{1,0:T(8,128)}, s32[]{:T(128)}, bf16[16,512,512]{2,1,0:T(8,128)(2,1)}, bf16[6144,256]{1,0:T(8,128)(2,1)S(1)}, f32[6144,256]{1,0:T(8,128)}) %tuple.128), branch_computations={%region_3.3_spmd, %region_4.5_spmd} | conditional | flops 134351360 | bytes 3422258 | solution.py:50
  70.6 8.9 scatter_fusion
  80.7 13.8 %conditional.6 = (f32[6144,256]{1,0:T(8,128)}) conditional(s32[]{:T(128)} %bitcast.62, f32[6144,256]{1,0:T(8,128)} %get-tuple-element.664, (s32[16,512]{1,0:T(8,128)}, s32[]{:T(128)}, bf16[16,512,512]{2,1,0:T(8,128)(2,1)}, bf16[6144,256]{1,0:T(8,128)(2,1)S(1)}, f32[6144,256]{1,0:T(8,128)}) %tuple.128), branch_computations={%region_3.3_spmd, %region_4.5_spmd} | conditional | flops 134351360 | bytes 3422258 | solution.py:50
  85.6 8.9 scatter_fusion
  95.7 13.8 %conditional.6 = (f32[6144,256]{1,0:T(8,128)}) conditional(s32[]{:T(128)} %bitcast.62, f32[6144,256]{1,0:T(8,128)} %get-tuple-element.664, (s32[16,512]{1,0:T(8,128)}, s32[]{:T(128)}, bf16[16,512,512]{2,1,0:T(8,128)(2,1)}, bf16[6144,256]{1,0:T(8,128)(2,1)S(1)}, f32[6144,256]{1,0:T(8,128)}) %tuple.128), branch_computations={%region_3.3_spmd, %region_4.5_spmd} | conditional | flops 134351360 | bytes 3422258 | solution.py:50
  100.6 8.9 scatter_fusion
  124.9 4.5 gather_fusion.6
  129.3 166.7 %collective-permute-start.2 = (f32[384,256]{1,0:T(8,128)S(1)}, f32[384,256]{1,0:T(8,128)S(1)}, u32[]{:S(2)}, u32[]{:S(2)}) collective-permute-start(f32[384,256]{1,0:T(8,128)S(1)} %gather_fusion.6), channel_id=1, source_target_pairs={{0,1},{1,2},{2,3},{3,4},{4,5},{5,6},{6,7},{7,8},{8,9},{9,10},{10,1... | collective-permute-start | bytes 1179656 | tf_op jit(solution)/shard_map/ppermute | solution.py:10
  296.1 4.5 gather_fusion.7
  302.3 7.8 scatter_fusion.4
  310.1 7.8 scatter_fusion.5
  318.0 5.8 multiply_convert_fusion.1
  323.8 3.1 broadcast.221.clone
  326.9 75.4 %while.50 = (s32[]{:T(128)}, f32[6144,256]{1,0:T(8,128)}, pred[16]{0:T(512)(128)(4,1)S(1)}, s32[16,512]{1,0:T(8,128)}, bf16[16,512,512]{2,1,0:T(8,128)(2,1)}, /*index=5*/bf16[6144,256]{1,0:T(8,128)(2,1)S(1)}, s32[]{:T(128)}) while((s32[]{:T(128)}, f32[6144,256]{1,0:T(8,128)}, pred[16]{0:T(512)(128)(4,1)S(1)}, s32[16,512]{1,0:T(8,128)}, ...), condition=%wide.region_13.14_spmd, body=%wide.region_9.13_spmd.sunk | while | flops 134351360 | bytes 3422386 | solution.py:52
  328.1 13.8 %conditional.7 = (f32[6144,256]{1,0:T(8,128)}) conditional(s32[]{:T(128)} %bitcast.63, f32[6144,256]{1,0:T(8,128)} %get-tuple-element.685, (s32[16,512]{1,0:T(8,128)}, s32[]{:T(128)}, bf16[16,512,512]{2,1,0:T(8,128)(2,1)}, bf16[6144,256]{1,0:T(8,128)(2,1)S(1)}, f32[6144,256]{1,0:T(8,128)}) %tuple.130), branch_computations={%region_10.10_spmd, %region_11.12_spmd} | conditional | flops 134351360 | bytes 3422258 | solution.py:50
  333.0 8.9 scatter_fusion.1
  343.1 13.8 %conditional.7 = (f32[6144,256]{1,0:T(8,128)}) conditional(s32[]{:T(128)} %bitcast.63, f32[6144,256]{1,0:T(8,128)} %get-tuple-element.685, (s32[16,512]{1,0:T(8,128)}, s32[]{:T(128)}, bf16[16,512,512]{2,1,0:T(8,128)(2,1)}, bf16[6144,256]{1,0:T(8,128)(2,1)S(1)}, f32[6144,256]{1,0:T(8,128)}) %tuple.130), branch_computations={%region_10.10_spmd, %region_11.12_spmd} | conditional | flops 134351360 | bytes 3422258 | solution.py:50
  348.0 8.9 scatter_fusion.1
  358.1 13.8 %conditional.7 = (f32[6144,256]{1,0:T(8,128)}) conditional(s32[]{:T(128)} %bitcast.63, f32[6144,256]{1,0:T(8,128)} %get-tuple-element.685, (s32[16,512]{1,0:T(8,128)}, s32[]{:T(128)}, bf16[16,512,512]{2,1,0:T(8,128)(2,1)}, bf16[6144,256]{1,0:T(8,128)(2,1)S(1)}, f32[6144,256]{1,0:T(8,128)}) %tuple.130), branch_computations={%region_10.10_spmd, %region_11.12_spmd} | conditional | flops 134351360 | bytes 3422258 | solution.py:50
  363.0 8.9 scatter_fusion.1
  373.1 13.8 %conditional.7 = (f32[6144,256]{1,0:T(8,128)}) conditional(s32[]{:T(128)} %bitcast.63, f32[6144,256]{1,0:T(8,128)} %get-tuple-element.685, (s32[16,512]{1,0:T(8,128)}, s32[]{:T(128)}, bf16[16,512,512]{2,1,0:T(8,128)(2,1)}, bf16[6144,256]{1,0:T(8,128)(2,1)S(1)}, f32[6144,256]{1,0:T(8,128)}) %tuple.130), branch_computations={%region_10.10_spmd, %region_11.12_spmd} | conditional | flops 134351360 | bytes 3422258 | solution.py:50
  378.0 8.9 scatter_fusion.1
  402.3 4.5 gather_fusion.8
  406.8 167.9 %collective-permute-start.4 = (f32[384,256]{1,0:T(8,128)S(1)}, f32[384,256]{1,0:T(8,128)S(1)}, u32[]{:S(2)}, u32[]{:S(2)}) collective-permute-start(f32[384,256]{1,0:T(8,128)S(1)} %gather_fusion.8), channel_id=1, source_target_pairs={{0,1},{1,2},{2,3},{3,4},{4,5},{5,6},{6,7},{7,8},{8,9},{9,10},{10,1... | collective-permute-start | bytes 1179656 | tf_op jit(solution)/shard_map/ppermute | solution.py:10
  574.7 4.5 gather_fusion.9
  580.5 8.0 scatter_fusion.6
  588.5 7.8 scatter_fusion.7
  596.3 7.5 multiply_convert_fusion
  603.8 3.1 broadcast.221
  606.9 75.5 %while.51 = (s32[]{:T(128)}, f32[6144,256]{1,0:T(8,128)}, pred[16]{0:T(512)(128)(4,1)S(1)}, s32[16,512]{1,0:T(8,128)}, bf16[16,512,512]{2,1,0:T(8,128)(2,1)}, /*index=5*/bf16[6144,256]{1,0:T(8,128)(2,1)S(1)}, s32[]{:T(128)}) while((s32[]{:T(128)}, f32[6144,256]{1,0:T(8,128)}, pred[16]{0:T(512)(128)(4,1)S(1)}, s32[16,512]{1,0:T(8,128)}, ...), condition=%wide.region_20.21_spmd, body=%wide.region_16.20_spmd.sunk | while | flops 134351360 | bytes 3422386 | solution.py:52
  608.1 13.8 %conditional.8 = (f32[6144,256]{1,0:T(8,128)}) conditional(s32[]{:T(128)} %bitcast.64, f32[6144,256]{1,0:T(8,128)} %get-tuple-element.706, (s32[16,512]{1,0:T(8,128)}, s32[]{:T(128)}, bf16[16,512,512]{2,1,0:T(8,128)(2,1)}, bf16[6144,256]{1,0:T(8,128)(2,1)S(1)}, f32[6144,256]{1,0:T(8,128)}) %tuple.132), branch_computations={%region_17.17_spmd, %region_18.19_spmd} | conditional | flops 134351360 | bytes 3422258 | solution.py:50
  613.0 9.0 scatter_fusion.2
  623.2 13.8 %conditional.8 = (f32[6144,256]{1,0:T(8,128)}) conditional(s32[]{:T(128)} %bitcast.64, f32[6144,256]{1,0:T(8,128)} %get-tuple-element.706, (s32[16,512]{1,0:T(8,128)}, s32[]{:T(128)}, bf16[16,512,512]{2,1,0:T(8,128)(2,1)}, bf16[6144,256]{1,0:T(8,128)(2,1)S(1)}, f32[6144,256]{1,0:T(8,128)}) %tuple.132), branch_computations={%region_17.17_spmd, %region_18.19_spmd} | conditional | flops 134351360 | bytes 3422258 | solution.py:50
  628.0 9.0 scatter_fusion.2
  638.2 13.8 %conditional.8 = (f32[6144,256]{1,0:T(8,128)}) conditional(s32[]{:T(128)} %bitcast.64, f32[6144,256]{1,0:T(8,128)} %get-tuple-element.706, (s32[16,512]{1,0:T(8,128)}, s32[]{:T(128)}, bf16[16,512,512]{2,1,0:T(8,128)(2,1)}, bf16[6144,256]{1,0:T(8,128)(2,1)S(1)}, f32[6144,256]{1,0:T(8,128)}) %tuple.132), branch_computations={%region_17.17_spmd, %region_18.19_spmd} | conditional | flops 134351360 | bytes 3422258 | solution.py:50
  643.1 9.0 scatter_fusion.2
  653.3 13.8 %conditional.8 = (f32[6144,256]{1,0:T(8,128)}) conditional(s32[]{:T(128)} %bitcast.64, f32[6144,256]{1,0:T(8,128)} %get-tuple-element.706, (s32[16,512]{1,0:T(8,128)}, s32[]{:T(128)}, bf16[16,512,512]{2,1,0:T(8,128)(2,1)}, bf16[6144,256]{1,0:T(8,128)(2,1)S(1)}, f32[6144,256]{1,0:T(8,128)}) %tuple.132), branch_computations={%region_17.17_spmd, %region_18.19_spmd} | conditional | flops 134351360 | bytes 3422258 | solution.py:50
  658.1 9.0 scatter_fusion.2
  682.4 4.5 gather_fusion.10
  686.9 4.5 gather_fusion.11
  691.4 168.4 %collective-permute-start.6 = (f32[384,256]{1,0:T(8,128)S(1)}, f32[384,256]{1,0:T(8,128)S(1)}, u32[]{:S(2)}, u32[]{:S(2)}) collective-permute-start(f32[384,256]{1,0:T(8,128)S(1)} %gather_fusion.10), channel_id=1, source_target_pairs={{0,1},{1,2},{2,3},{3,4},{4,5},{5,6},{6,7},{7,8},{8,9},{9,10},{10,1... | collective-permute-start | bytes 1179656 | tf_op jit(solution)/shard_map/ppermute | solution.py:10
  863.8 7.9 scatter_fusion.8
  871.7 7.9 scatter_fusion.9
  879.6 9.7 multiply_subtract_fusion
  889.3 2.7 copy-done
  892.0 12.9 %fusion.13 = f32[256,256]{0,1:T(8,128)} fusion(f32[6144,256]{1,0:T(8,128)S(1)} %multiply_subtract_fusion, pred[6144]{0:T(1024)(128)(4,1)S(1)} %not_and_fusion), kind=kOutput, calls=%fused_computation.47 | convolution fusion | flops 4833411072 | bytes 6559744 | tf_op jit(solution)/shard_map/dot_general | solution.py:67
  906.2 132.1 %all-reduce.3.cloned.1.call-done = f32[256,256]{0,1:T(8,128)} async-done(((f32[256,256]{0,1:T(8,128)}), f32[256,256]{0,1:T(8,128)}) %all-reduce.3.cloned.1.call-update) | async-done | bytes 262160 | tf_op jit(solution)/shard_map/psum | solution.py:74
  1040.8 11.7 %cholesky.50 = f32[128,128]{1,0:T(8,128)S(1)} custom-call(f32[128,128]{1,0:T(8,128)S(1)} %cholesky.118), custom_call_target="Cholesky" | custom-call | tf_op jit(solution)/shard_map/jit(cholesky)/cholesky | solution.py:77
  1052.6 9.8 custom-call.15
  1062.8 11.7 %cholesky.105 = f32[128,128]{1,0:T(8,128)S(1)} custom-call(f32[128,128]{1,0:T(8,128)S(1)} %convolution_subtract_fusion.1), custom_call_target="Cholesky" | custom-call | tf_op jit(solution)/shard_map/jit(cholesky)/cholesky | solution.py:77
  1076.6 3.8 while.52
  1080.4 19.8 %custom-call.16 = f32[2,128,128]{1,2,0:T(8,128)S(1)} custom-call(f32[2,128,128]{2,1,0:T(8,128)S(1)} %get-tuple-element.459), custom_call_target="InvertDiagBlocksLowerTriangular" | custom-call | tf_op jit(solution)/shard_map/jit(_solve_triangular)/triangular_solve | solution.py:78
  1101.1 8.9 convolution_select_fusion
  (189 shorter events, 109.3 us)
Async XLA Ops:
  6.5 1031.7 %all-reduce.3.cloned.1.call-start = ((), (), s32[]{:S(2)}) async-start(), calls=%async_computation | async-start | bytes 524288 | tf_op jit(solution)/shard_map/psum | solution.py:74
  7.3 5.8 copy-start.1
  15.7 14.6 %collective-permute-start = (f32[384]{0:T(512)S(1)}, f32[384]{0:T(512)S(1)}, u32[]{:S(2)}, u32[]{:S(2)}) collective-permute-start(f32[384]{0:T(512)S(1)} %gather_fusion.3), channel_id=1, source_target_pairs={{0,1},{1,2},{2,3},{3,4},{4,5},{5,6},{6,7},{7,8},{8,9},{9,10},{10,1... | collective-permute-start | bytes 4616 | tf_op jit(solution)/shard_map/ppermute | solution.py:10
  22.5 10.8 collective-permute-start.1
  129.3 173.0 %collective-permute-start.2 = (f32[384,256]{1,0:T(8,128)S(1)}, f32[384,256]{1,0:T(8,128)S(1)}, u32[]{:S(2)}, u32[]{:S(2)}) collective-permute-start(f32[384,256]{1,0:T(8,128)S(1)} %gather_fusion.6), channel_id=1, source_target_pairs={{0,1},{1,2},{2,3},{3,4},{4,5},{5,6},{6,7},{7,8},{8,9},{9,10},{10,1... | collective-permute-start | bytes 1179656 | tf_op jit(solution)/shard_map/ppermute | solution.py:10
  300.5 9.6 collective-permute-start.3
  406.8 173.7 %collective-permute-start.4 = (f32[384,256]{1,0:T(8,128)S(1)}, f32[384,256]{1,0:T(8,128)S(1)}, u32[]{:S(2)}, u32[]{:S(2)}) collective-permute-start(f32[384,256]{1,0:T(8,128)S(1)} %gather_fusion.8), channel_id=1, source_target_pairs={{0,1},{1,2},{2,3},{3,4},{4,5},{5,6},{6,7},{7,8},{8,9},{9,10},{10,1... | collective-permute-start | bytes 1179656 | tf_op jit(solution)/shard_map/ppermute | solution.py:10
  579.1 9.3 collective-permute-start.5
  682.4 179.5 %copy-start.2 = (s32[32]{0:T(128)S(1)}, s32[32]{0:T(128)}, u32[]{:S(2)}) copy-start(s32[32]{0:T(128)} %param.24) | copy-start | bytes 388
  691.4 172.4 %collective-permute-start.6 = (f32[384,256]{1,0:T(8,128)S(1)}, f32[384,256]{1,0:T(8,128)S(1)}, u32[]{:S(2)}, u32[]{:S(2)}) collective-permute-start(f32[384,256]{1,0:T(8,128)S(1)} %gather_fusion.10), channel_id=1, source_target_pairs={{0,1},{1,2},{2,3},{3,4},{4,5},{5,6},{6,7},{7,8},{8,9},{9,10},{10,1... | collective-permute-start | bytes 1179656 | tf_op jit(solution)/shard_map/ppermute | solution.py:10
  859.7 12.0 %collective-permute-start.7 = (f32[384,256]{1,0:T(8,128)S(1)}, f32[384,256]{1,0:T(8,128)S(1)}, u32[]{:S(2)}, u32[]{:S(2)}) collective-permute-start(f32[384,256]{1,0:T(8,128)S(1)} %gather_fusion.11), channel_id=1, source_target_pairs={{1,0},{2,1},{3,2},{4,3},{5,4},{6,5},{7,6},{8,7},{9,8},{10,9},{11,1... | collective-permute-start | bytes 1179656 | tf_op jit(solution)/shard_map/ppermute | solution.py:10
  889.3 2.7 copy-start
Sparse Core Ops, SparseCore 0:
  905.0 133.2 all-reduce.2
where the time goes:
time: 1140 us; the launch traced here: 1120 us
  starting transfers between devices  514 us (45%)
  other arithmetic  258 us (23%)
  waiting for transfers between devices  132 us (12%)
  local copies, waits for them, and re-layouts  115 us (10%)
  matrix products  48.7 us (4%)
  loops' own time  32.5 us (3%)
  between operations  16.5 us (1%)
    ppermute x8, starting transfers between devices, passed_along(): return lax.ppermute(block, axis, route)  514 us
    psum x1, waiting for transfers between devices, body(): gram = lax.psum(partial_value, 'mesh')  132 us
    scatter-add x12, other arithmetic, compute(): return acc.at[rows].add(part)  107 us
    scatter-add x6, other arithmetic, ham(): local.at[lower_rows].add(coming_up).at[upper_rows].add(coming_down)  47.2 us
    another operation x6, other arithmetic, body(): factor = jnp.linalg.cholesky(gram)  34 us
    another operation x3, loops' own time, ham(): local = lax.fori_loop(0, slots, add_element, empty)  31.5 us
    dynamic_slice x48, local copies, waits for them, and re-layouts, add_element(): return lax.cond(slot_live[slot], compute, lambda acc: acc, total)  28.8 us
    dot_general x12, matrix products, compute(): jnp.dot(element_blocks[slot], scaled[rows], preferred_element_type=jnp.fl...  25.6 us
  transfers between devices with their start and end apart: 9, of which 1 were waited for; matrix products, arithmetic and copies ran while one was open for 4% of the time, Pallas kernels for 0%

commit v1 on v0

--- a/solution.py
+++ b/solution.py
@@ -1,7 +1,20 @@
+import functools
 import jax
 import jax.numpy as jnp
 from jax import lax
 from jax.sharding import PartitionSpec as P
+from jax.lax import axis_size, ppermute
+
+
+def digits_place(in_array, bus_axis):
+    response = in_array
+    extent = axis_size(bus_axis)
+    for u in [[(it, it ^ d) for it in range(extent)] for d in (1, 2, 4, 8, 16) if d < extent]:
+        response = response + ppermute(response, bus_axis, perm=u)
+    return response
+
+
+kinds_set = functools.partial(digits_place, bus_axis="mesh")
 
 
 def passed_along(block, axis, distance):
@@ -71,7 +84,7 @@
         precision=lax.Precision.HIGHEST,
         preferred_element_type=jnp.float32,
     )
-    gram = lax.psum(partial_value, "mesh")
+    gram = kinds_set(partial_value)
     total = (jnp.sum(node_counts) - shared * (devices - 1)).astype(jnp.float32)
     gram = gram / total
     factor = jnp.linalg.cholesky(gram)

time: 1140 us -> 1030 us (0.904)
  waiting for transfers between devices: 132 us -> 31.6 us
  between operations: 16.5 us -> 3.47 us
  starting transfers between devices: 514 us -> 527 us
    psum x1 -> x0, waiting for transfers between devices: 132 us -> none  [body(): gram = lax.psum(partial_value, 'mesh')]
    ppermute x0 -> x5, waiting for transfers between devices: none -> 31.6 us  [digits_place(): response = response + ppermute(response, bus_axis, perm=u)]
    ppermute x0 -> x5, starting transfers between devices: none -> 13.2 us  [digits_place(): response = response + ppermute(response, bus_axis, perm=u)]
  transfers between devices with their start and end apart: 9 -> 13, of which waited for: 1 -> 5; matrix products, arithmetic and copies ran while one was open for 4% -> 5% of each run, Pallas kernels for 0% -> 0%
where the time goes in v1:
time: 1030 us; the launch traced here: 1010 us
  starting transfers between devices  527 us (51%)
  other arithmetic  257 us (25%)
  local copies, waits for them, and re-layouts  115 us (11%)
  matrix products  48.2 us (5%)
  loops' own time  32.5 us (3%)
  waiting for transfers between devices  31.6 us (3%)
    ppermute x8, starting transfers between devices, passed_along(): return lax.ppermute(block, axis, route)  514 us
    scatter-add x12, other arithmetic, compute(): return acc.at[rows].add(part)  107 us
    scatter-add x6, other arithmetic, ham(): local.at[lower_rows].add(coming_up).at[upper_rows].add(coming_down)  47.4 us
    another operation x6, other arithmetic, body(): factor = jnp.linalg.cholesky(gram)  34 us
    ppermute x5, waiting for transfers between devices, digits_place(): response = response + ppermute(response, bus_axis, perm=u)  31.6 us
    another operation x3, loops' own time, ham(): local = lax.fori_loop(0, slots, add_element, empty)  31.5 us
    dynamic_slice x48, local copies, waits for them, and re-layouts, add_element(): return lax.cond(slot_live[slot], compute, lambda acc: acc, total)  28.8 us
    dot_general x12, matrix products, compute(): jnp.dot(element_blocks[slot], scaled[rows], preferred_element_type=jnp.fl...  25.6 us
  transfers between devices with their start and end apart: 13, of which 5 were waited for; matrix products, arithmetic and copies ran while one was open for 5% of the time, Pallas kernels for 0%

profile of v1, /device:TPU:0, one launch (start us, length us, event | category | flops | bytes accessed | tf_op | source)
XLA Modules:
  0.0 1013.9 jit_solution(13592414409181475433)
XLA Ops:
  0.7 5.8 copy.68
  11.5 4.4 gather_fusion.5
  16.0 4.5 collective-permute-start.1
  26.8 9.7 scatter_custom_fusion.4
  36.5 3.3 multiply_convert_fusion.2
  42.9 75.4 %while.49 = (s32[]{:T(128)}, f32[6144,256]{1,0:T(8,128)}, pred[16]{0:T(512)(128)(4,1)S(1)}, s32[16,512]{1,0:T(8,128)}, bf16[16,512,512]{2,1,0:T(8,128)(2,1)}, /*index=5*/bf16[6144,256]{1,0:T(8,128)(2,1)S(1)}, s32[]{:T(128)}) while((s32[]{:T(128)}, f32[6144,256]{1,0:T(8,128)}, pred[16]{0:T(512)(128)(4,1)S(1)}, s32[16,512]{1,0:T(8,128)}, ...), condition=%wide.region_6.7_spmd, body=%wide.region_2.6_spmd.sunk | while | flops 134351360 | bytes 3422386 | solution.py:65
  44.1 13.8 %conditional.6 = (f32[6144,256]{1,0:T(8,128)}) conditional(s32[]{:T(128)} %bitcast.62, f32[6144,256]{1,0:T(8,128)} %get-tuple-element.664, (s32[16,512]{1,0:T(8,128)}, s32[]{:T(128)}, bf16[16,512,512]{2,1,0:T(8,128)(2,1)}, bf16[6144,256]{1,0:T(8,128)(2,1)S(1)}, f32[6144,256]{1,0:T(8,128)}) %tuple.128), branch_computations={%region_3.3_spmd, %region_4.5_spmd} | conditional | flops 134351360 | bytes 3422258 | solution.py:63
  49.0 8.9 scatter_fusion
  59.2 13.8 %conditional.6 = (f32[6144,256]{1,0:T(8,128)}) conditional(s32[]{:T(128)} %bitcast.62, f32[6144,256]{1,0:T(8,128)} %get-tuple-element.664, (s32[16,512]{1,0:T(8,128)}, s32[]{:T(128)}, bf16[16,512,512]{2,1,0:T(8,128)(2,1)}, bf16[6144,256]{1,0:T(8,128)(2,1)S(1)}, f32[6144,256]{1,0:T(8,128)}) %tuple.128), branch_computations={%region_3.3_spmd, %region_4.5_spmd} | conditional | flops 134351360 | bytes 3422258 | solution.py:63
  64.0 8.9 scatter_fusion
  74.2 13.8 %conditional.6 = (f32[6144,256]{1,0:T(8,128)}) conditional(s32[]{:T(128)} %bitcast.62, f32[6144,256]{1,0:T(8,128)} %get-tuple-element.664, (s32[16,512]{1,0:T(8,128)}, s32[]{:T(128)}, bf16[16,512,512]{2,1,0:T(8,128)(2,1)}, bf16[6144,256]{1,0:T(8,128)(2,1)S(1)}, f32[6144,256]{1,0:T(8,128)}) %tuple.128), branch_computations={%region_3.3_spmd, %region_4.5_spmd} | conditional | flops 134351360 | bytes 3422258 | solution.py:63
  79.0 8.9 scatter_fusion
  89.2 13.8 %conditional.6 = (f32[6144,256]{1,0:T(8,128)}) conditional(s32[]{:T(128)} %bitcast.62, f32[6144,256]{1,0:T(8,128)} %get-tuple-element.664, (s32[16,512]{1,0:T(8,128)}, s32[]{:T(128)}, bf16[16,512,512]{2,1,0:T(8,128)(2,1)}, bf16[6144,256]{1,0:T(8,128)(2,1)S(1)}, f32[6144,256]{1,0:T(8,128)}) %tuple.128), branch_computations={%region_3.3_spmd, %region_4.5_spmd} | conditional | flops 134351360 | bytes 3422258 | solution.py:63
  94.1 8.9 scatter_fusion
  118.3 4.5 gather_fusion.6
  122.8 166.7 %collective-permute-start.2 = (f32[384,256]{1,0:T(8,128)S(1)}, f32[384,256]{1,0:T(8,128)S(1)}, u32[]{:S(2)}, u32[]{:S(2)}) collective-permute-start(f32[384,256]{1,0:T(8,128)S(1)} %gather_fusion.6), channel_id=1, source_target_pairs={{0,1},{1,2},{2,3},{3,4},{4,5},{5,6},{6,7},{7,8},{8,9},{9,10},{10,1... | collective-permute-start | bytes 1179656 | tf_op jit(solution)/shard_map/ppermute | solution.py:23
  289.5 4.5 gather_fusion.7
  295.5 7.8 scatter_fusion.4
  303.3 7.8 scatter_fusion.5
  311.1 5.8 multiply_convert_fusion.1
  317.0 3.1 broadcast.221.clone
  320.0 75.4 %while.50 = (s32[]{:T(128)}, f32[6144,256]{1,0:T(8,128)}, pred[16]{0:T(512)(128)(4,1)S(1)}, s32[16,512]{1,0:T(8,128)}, bf16[16,512,512]{2,1,0:T(8,128)(2,1)}, /*index=5*/bf16[6144,256]{1,0:T(8,128)(2,1)S(1)}, s32[]{:T(128)}) while((s32[]{:T(128)}, f32[6144,256]{1,0:T(8,128)}, pred[16]{0:T(512)(128)(4,1)S(1)}, s32[16,512]{1,0:T(8,128)}, ...), condition=%wide.region_13.14_spmd, body=%wide.region_9.13_spmd.sunk | while | flops 134351360 | bytes 3422386 | solution.py:65
  321.3 13.8 %conditional.7 = (f32[6144,256]{1,0:T(8,128)}) conditional(s32[]{:T(128)} %bitcast.63, f32[6144,256]{1,0:T(8,128)} %get-tuple-element.685, (s32[16,512]{1,0:T(8,128)}, s32[]{:T(128)}, bf16[16,512,512]{2,1,0:T(8,128)(2,1)}, bf16[6144,256]{1,0:T(8,128)(2,1)S(1)}, f32[6144,256]{1,0:T(8,128)}) %tuple.130), branch_computations={%region_10.10_spmd, %region_11.12_spmd} | conditional | flops 134351360 | bytes 3422258 | solution.py:63
  326.1 8.9 scatter_fusion.1
  336.3 13.8 %conditional.7 = (f32[6144,256]{1,0:T(8,128)}) conditional(s32[]{:T(128)} %bitcast.63, f32[6144,256]{1,0:T(8,128)} %get-tuple-element.685, (s32[16,512]{1,0:T(8,128)}, s32[]{:T(128)}, bf16[16,512,512]{2,1,0:T(8,128)(2,1)}, bf16[6144,256]{1,0:T(8,128)(2,1)S(1)}, f32[6144,256]{1,0:T(8,128)}) %tuple.130), branch_computations={%region_10.10_spmd, %region_11.12_spmd} | conditional | flops 134351360 | bytes 3422258 | solution.py:63
  341.1 8.9 scatter_fusion.1
  351.3 13.8 %conditional.7 = (f32[6144,256]{1,0:T(8,128)}) conditional(s32[]{:T(128)} %bitcast.63, f32[6144,256]{1,0:T(8,128)} %get-tuple-element.685, (s32[16,512]{1,0:T(8,128)}, s32[]{:T(128)}, bf16[16,512,512]{2,1,0:T(8,128)(2,1)}, bf16[6144,256]{1,0:T(8,128)(2,1)S(1)}, f32[6144,256]{1,0:T(8,128)}) %tuple.130), branch_computations={%region_10.10_spmd, %region_11.12_spmd} | conditional | flops 134351360 | bytes 3422258 | solution.py:63
  356.2 8.9 scatter_fusion.1
  366.3 13.8 %conditional.7 = (f32[6144,256]{1,0:T(8,128)}) conditional(s32[]{:T(128)} %bitcast.63, f32[6144,256]{1,0:T(8,128)} %get-tuple-element.685, (s32[16,512]{1,0:T(8,128)}, s32[]{:T(128)}, bf16[16,512,512]{2,1,0:T(8,128)(2,1)}, bf16[6144,256]{1,0:T(8,128)(2,1)S(1)}, f32[6144,256]{1,0:T(8,128)}) %tuple.130), branch_computations={%region_10.10_spmd, %region_11.12_spmd} | conditional | flops 134351360 | bytes 3422258 | solution.py:63
  371.2 8.9 scatter_fusion.1
  395.5 4.5 gather_fusion.8
  399.9 167.9 %collective-permute-start.4 = (f32[384,256]{1,0:T(8,128)S(1)}, f32[384,256]{1,0:T(8,128)S(1)}, u32[]{:S(2)}, u32[]{:S(2)}) collective-permute-start(f32[384,256]{1,0:T(8,128)S(1)} %gather_fusion.8), channel_id=1, source_target_pairs={{0,1},{1,2},{2,3},{3,4},{4,5},{5,6},{6,7},{7,8},{8,9},{9,10},{10,1... | collective-permute-start | bytes 1179656 | tf_op jit(solution)/shard_map/ppermute | solution.py:23
  567.9 4.5 gather_fusion.9
  574.3 8.2 scatter_fusion.6
  582.5 7.8 scatter_fusion.7
  590.3 7.5 multiply_convert_fusion
  597.8 3.1 broadcast.221
  600.9 75.5 %while.51 = (s32[]{:T(128)}, f32[6144,256]{1,0:T(8,128)}, pred[16]{0:T(512)(128)(4,1)S(1)}, s32[16,512]{1,0:T(8,128)}, bf16[16,512,512]{2,1,0:T(8,128)(2,1)}, /*index=5*/bf16[6144,256]{1,0:T(8,128)(2,1)S(1)}, s32[]{:T(128)}) while((s32[]{:T(128)}, f32[6144,256]{1,0:T(8,128)}, pred[16]{0:T(512)(128)(4,1)S(1)}, s32[16,512]{1,0:T(8,128)}, ...), condition=%wide.region_20.21_spmd, body=%wide.region_16.20_spmd.sunk | while | flops 134351360 | bytes 3422386 | solution.py:65
  602.2 13.8 %conditional.8 = (f32[6144,256]{1,0:T(8,128)}) conditional(s32[]{:T(128)} %bitcast.64, f32[6144,256]{1,0:T(8,128)} %get-tuple-element.706, (s32[16,512]{1,0:T(8,128)}, s32[]{:T(128)}, bf16[16,512,512]{2,1,0:T(8,128)(2,1)}, bf16[6144,256]{1,0:T(8,128)(2,1)S(1)}, f32[6144,256]{1,0:T(8,128)}) %tuple.132), branch_computations={%region_17.17_spmd, %region_18.19_spmd} | conditional | flops 134351360 | bytes 3422258 | solution.py:63
  607.0 9.0 scatter_fusion.2
  617.2 13.8 %conditional.8 = (f32[6144,256]{1,0:T(8,128)}) conditional(s32[]{:T(128)} %bitcast.64, f32[6144,256]{1,0:T(8,128)} %get-tuple-element.706, (s32[16,512]{1,0:T(8,128)}, s32[]{:T(128)}, bf16[16,512,512]{2,1,0:T(8,128)(2,1)}, bf16[6144,256]{1,0:T(8,128)(2,1)S(1)}, f32[6144,256]{1,0:T(8,128)}) %tuple.132), branch_computations={%region_17.17_spmd, %region_18.19_spmd} | conditional | flops 134351360 | bytes 3422258 | solution.py:63
  622.1 9.0 scatter_fusion.2
  632.3 13.8 %conditional.8 = (f32[6144,256]{1,0:T(8,128)}) conditional(s32[]{:T(128)} %bitcast.64, f32[6144,256]{1,0:T(8,128)} %get-tuple-element.706, (s32[16,512]{1,0:T(8,128)}, s32[]{:T(128)}, bf16[16,512,512]{2,1,0:T(8,128)(2,1)}, bf16[6144,256]{1,0:T(8,128)(2,1)S(1)}, f32[6144,256]{1,0:T(8,128)}) %tuple.132), branch_computations={%region_17.17_spmd, %region_18.19_spmd} | conditional | flops 134351360 | bytes 3422258 | solution.py:63
  637.1 9.0 scatter_fusion.2
  647.3 13.8 %conditional.8 = (f32[6144,256]{1,0:T(8,128)}) conditional(s32[]{:T(128)} %bitcast.64, f32[6144,256]{1,0:T(8,128)} %get-tuple-element.706, (s32[16,512]{1,0:T(8,128)}, s32[]{:T(128)}, bf16[16,512,512]{2,1,0:T(8,128)(2,1)}, bf16[6144,256]{1,0:T(8,128)(2,1)S(1)}, f32[6144,256]{1,0:T(8,128)}) %tuple.132), branch_computations={%region_17.17_spmd, %region_18.19_spmd} | conditional | flops 134351360 | bytes 3422258 | solution.py:63
  652.2 9.0 scatter_fusion.2
  676.4 4.5 gather_fusion.10
  680.9 4.5 gather_fusion.11
  685.4 168.4 %collective-permute-start.6 = (f32[384,256]{1,0:T(8,128)S(1)}, f32[384,256]{1,0:T(8,128)S(1)}, u32[]{:S(2)}, u32[]{:S(2)}) collective-permute-start(f32[384,256]{1,0:T(8,128)S(1)} %gather_fusion.10), channel_id=1, source_target_pairs={{0,1},{1,2},{2,3},{3,4},{4,5},{5,6},{6,7},{7,8},{8,9},{9,10},{10,1... | collective-permute-start | bytes 1179656 | tf_op jit(solution)/shard_map/ppermute | solution.py:23
  856.6 7.9 scatter_fusion.8
  864.5 7.9 scatter_fusion.9
  872.3 9.7 multiply_subtract_fusion
  884.7 12.4 %fusion.13 = f32[256,256]{0,1:T(8,128)S(1)} fusion(f32[6144,256]{1,0:T(8,128)S(1)} %multiply_subtract_fusion, pred[6144]{0:T(1024)(128)(4,1)S(1)} %not_and_fusion), kind=kOutput, calls=%fused_computation.47 | convolution fusion | flops 4833411072 | bytes 6559744 | tf_op jit(solution)/shard_map/dot_general | solution.py:80
  903.0 6.6 collective-permute-done.9
  909.7 7.8 collective-permute-done.10
  917.5 8.3 collective-permute-start.11
  925.8 5.2 collective-permute-done.11
  933.1 10.9 %collective-permute-done.12 = f32[256,256]{0,1:T(8,128)S(1)} collective-permute-done((f32[256,256]{0,1:T(8,128)S(1)}, f32[256,256]{0,1:T(8,128)S(1)}, u32[]{:S(2)}, u32[]{:S(2)}) %collective-permute-start.12) | collective-permute-done | bytes 262176 | tf_op jit(solution)/shard_map/ppermute | solution.py:13
  944.2 11.7 %cholesky.50 = f32[128,128]{1,0:T(8,128)S(1)} custom-call(f32[128,128]{1,0:T(8,128)S(1)} %cholesky.118), custom_call_target="Cholesky" | custom-call | tf_op jit(solution)/shard_map/jit(cholesky)/cholesky | solution.py:90
  955.9 9.8 custom-call.15
  966.2 11.7 %cholesky.105 = f32[128,128]{1,0:T(8,128)S(1)} custom-call(f32[128,128]{1,0:T(8,128)S(1)} %convolution_subtract_fusion.1), custom_call_target="Cholesky" | custom-call | tf_op jit(solution)/shard_map/jit(cholesky)/cholesky | solution.py:90
  980.0 3.8 while.52
  983.8 19.9 %custom-call.16 = f32[2,128,128]{1,2,0:T(8,128)S(1)} custom-call(f32[2,128,128]{2,1,0:T(8,128)S(1)} %get-tuple-element.459), custom_call_target="InvertDiagBlocksLowerTriangular" | custom-call | tf_op jit(solution)/shard_map/jit(_solve_triangular)/triangular_solve | solution.py:91
  1004.6 8.9 convolution_select_fusion
  (200 shorter events, 124.0 us)
Async XLA Ops:
  0.7 5.8 copy-start.1
  9.1 14.6 %collective-permute-start = (f32[384]{0:T(512)S(1)}, f32[384]{0:T(512)S(1)}, u32[]{:S(2)}, u32[]{:S(2)}) collective-permute-start(f32[384]{0:T(512)S(1)} %gather_fusion.3), channel_id=1, source_target_pairs={{0,1},{1,2},{2,3},{3,4},{4,5},{5,6},{6,7},{7,8},{8,9},{9,10},{10,1... | collective-permute-start | bytes 4616 | tf_op jit(solution)/shard_map/ppermute | solution.py:23
  16.0 10.8 %collective-permute-start.1 = (f32[384,256]{1,0:T(8,128)S(1)}, f32[384,256]{1,0:T(8,128)S(1)}, u32[]{:S(2)}, u32[]{:S(2)}) collective-permute-start(f32[384,256]{1,0:T(8,128)S(1)} %gather_fusion.5), channel_id=1, source_target_pairs={{0,1},{1,2},{2,3},{3,4},{4,5},{5,6},{6,7},{7,8},{8,9},{9,10},{10,1... | collective-permute-start | bytes 1179656 | tf_op jit(solution)/shard_map/ppermute | solution.py:23
  122.8 172.7 %collective-permute-start.2 = (f32[384,256]{1,0:T(8,128)S(1)}, f32[384,256]{1,0:T(8,128)S(1)}, u32[]{:S(2)}, u32[]{:S(2)}) collective-permute-start(f32[384,256]{1,0:T(8,128)S(1)} %gather_fusion.6), channel_id=1, source_target_pairs={{0,1},{1,2},{2,3},{3,4},{4,5},{5,6},{6,7},{7,8},{8,9},{9,10},{10,1... | collective-permute-start | bytes 1179656 | tf_op jit(solution)/shard_map/ppermute | solution.py:23
  294.0 9.3 collective-permute-start.3
  395.5 178.2 %copy-start.2 = (s32[32]{0:T(128)S(1)}, s32[32]{0:T(128)}, u32[]{:S(2)}) copy-start(s32[32]{0:T(128)} %param.24) | copy-start | bytes 388
  399.9 174.3 %collective-permute-start.4 = (f32[384,256]{1,0:T(8,128)S(1)}, f32[384,256]{1,0:T(8,128)S(1)}, u32[]{:S(2)}, u32[]{:S(2)}) collective-permute-start(f32[384,256]{1,0:T(8,128)S(1)} %gather_fusion.8), channel_id=1, source_target_pairs={{0,1},{1,2},{2,3},{3,4},{4,5},{5,6},{6,7},{7,8},{8,9},{9,10},{10,1... | collective-permute-start | bytes 1179656 | tf_op jit(solution)/shard_map/ppermute | solution.py:23
  572.3 10.2 %collective-permute-start.5 = (f32[384,256]{1,0:T(8,128)S(1)}, f32[384,256]{1,0:T(8,128)S(1)}, u32[]{:S(2)}, u32[]{:S(2)}) collective-permute-start(f32[384,256]{1,0:T(8,128)S(1)} %gather_fusion.9), channel_id=1, source_target_pairs={{1,0},{2,1},{3,2},{4,3},{5,4},{6,5},{7,6},{8,7},{9,8},{10,9},{11,1... | collective-permute-start | bytes 1179656 | tf_op jit(solution)/shard_map/ppermute | solution.py:23
  685.4 171.2 %collective-permute-start.6 = (f32[384,256]{1,0:T(8,128)S(1)}, f32[384,256]{1,0:T(8,128)S(1)}, u32[]{:S(2)}, u32[]{:S(2)}) collective-permute-start(f32[384,256]{1,0:T(8,128)S(1)} %gather_fusion.10), channel_id=1, source_target_pairs={{0,1},{1,2},{2,3},{3,4},{4,5},{5,6},{6,7},{7,8},{8,9},{9,10},{10,1... | collective-permute-start | bytes 1179656 | tf_op jit(solution)/shard_map/ppermute | solution.py:23
  853.7 10.7 %collective-permute-start.7 = (f32[384,256]{1,0:T(8,128)S(1)}, f32[384,256]{1,0:T(8,128)S(1)}, u32[]{:S(2)}, u32[]{:S(2)}) collective-permute-start(f32[384,256]{1,0:T(8,128)S(1)} %gather_fusion.11), channel_id=1, source_target_pairs={{1,0},{2,1},{3,2},{4,3},{5,4},{6,5},{7,6},{8,7},{9,8},{10,9},{11,1... | collective-permute-start | bytes 1179656 | tf_op jit(solution)/shard_map/ppermute | solution.py:23
  882.0 2.7 copy-start
  897.1 3.1 collective-permute-start.8
  900.2 9.4 collective-permute-start.9
  909.6 7.8 collective-permute-start.10
  917.5 13.5 %collective-permute-start.11 = (f32[256,256]{0,1:T(8,128)S(1)}, f32[256,256]{0,1:T(8,128)S(1)}, u32[]{:S(2)}, u32[]{:S(2)}) collective-permute-start(f32[256,256]{0,1:T(8,128)S(1)} %add.209), channel_id=1, source_target_pairs={{0,8},{1,9},{2,10},{3,11},{4,12},{5,13},{6,14},{7,15},{8,0},{9,1},... | collective-permute-start | bytes 786440 | tf_op jit(solution)/shard_map/ppermute | solution.py:13
  931.0 12.9 %collective-permute-start.12 = (f32[256,256]{0,1:T(8,128)S(1)}, f32[256,256]{0,1:T(8,128)S(1)}, u32[]{:S(2)}, u32[]{:S(2)}) collective-permute-start(f32[256,256]{0,1:T(8,128)S(1)} %add.210), channel_id=1, source_target_pairs={{0,16},{1,17},{2,18},{3,19},{4,20},{5,21},{6,22},{7,23},{8,24},{9,... | collective-permute-start | bytes 786440 | tf_op jit(solution)/shard_map/ppermute | solution.py:13
